TPU v7x, 256 devices: a whole 4x4x8 slice. The times are simulated.
256 devices in a mesh: tm: 32 (over x_hi, z, core), stripe: 8 (over x_lo, y).
Axes of the slice: x: 4 (x_hi: 2, x_lo: 2; x = x_hi * 2 + x_lo), y: 4, z: 8, core: 2. Of those that a mesh axis runs over, the one named last changes fastest.
Arguments:
- data_vec: float32 [128, 2, 512], P('tm', None, 'stripe'), may hold values from -6 to 6
- kernel: bfloat16 [128, 2, 512, 8192], P('tm', None, None, 'stripe'), may hold values from -0.1875 to 0.1875
- time_spectrum: float32 [128], P('tm'), may hold values from 0.25 to 2
- prior_spectrum: float32 [128, 64], replicated, may hold values from 0.05 to 1
- noise_var: float32 [512], P('stripe'), may hold values from 0.1 to 1
Outputs:
- hessian_vec: float32 [128, 2, 512], P('tm', None, 'stripe')
All inputs are finite; a program needn't handle non-finite values.
Results may differ from a plain program's by a relative error of at most 0.0022.
Values may be sent and summed in bfloat16 or wider, within the bound.
No kernel may reach another device: no remote copies, remote signals or barrier semaphores. Data moves between devices by JAX's collectives and lax.ppermute only.
A program may use at most 64 MiB of HBM per device.

v0:
```python
import math
import jax
import jax.numpy as jnp
from jax import lax
from jax.sharding import PartitionSpec as P

precise = lax.Precision.HIGHEST


def angle_tables(freq_ids, time_ids, length):
    product = freq_ids[:, None] * time_ids[None, :] % (2 * length)
    angles = product.astype(jnp.float32) * (math.pi / length)
    return (jnp.cos(angles), jnp.sin(angles))


def sine_matrix(length):
    numbers = jnp.arange(length, dtype=jnp.int32) + 1
    product = numbers[:, None] * numbers[None, :] % (2 * (length + 1))
    return jnp.sin(product.astype(jnp.float32) * (math.pi / (length + 1))) * math.sqrt(
        2.0 / (length + 1)
    )


def spectra_term(values, tm_index, time_total, count):
    steps_here = values.shape[0]
    freq_ids = jnp.arange(count, dtype=jnp.int32)
    time_ids = tm_index * steps_here + jnp.arange(steps_here, dtype=jnp.int32)
    cosine, sine_part = angle_tables(freq_ids, time_ids, time_total)
    real_part = jnp.einsum("kt,tns->kns", cosine, values, precision=precise)
    imag_part = -jnp.einsum("kt,tns->kns", sine_part, values, precision=precise)
    return jnp.stack([real_part, imag_part], 1) / math.sqrt(time_total)


def times_term(images, tm_index, time_total, count):
    freqs_here = images.shape[0]
    time_ids = jnp.arange(count, dtype=jnp.int32)
    freq_ids = tm_index * freqs_here + jnp.arange(freqs_here, dtype=jnp.int32)
    cosine, sine_part = angle_tables(freq_ids, time_ids, time_total)
    time_real = jnp.einsum("kt,kns->tns", cosine, images[:, 0], precision=precise)
    time_imag = jnp.einsum("kt,kns->tns", sine_part, images[:, 1], precision=precise)
    return (time_real - time_imag) / math.sqrt(time_total)


def grid_prior(grid_stack, row_sine, column_sine, spectrum):
    forward_grid = jnp.einsum("ai,mij->maj", row_sine, grid_stack, precision=precise)
    forward_grid = (
        jnp.einsum("maj,jb->mab", forward_grid, column_sine, precision=precise) * spectrum
    )
    backward_grid = jnp.einsum("ia,mab->mib", row_sine, forward_grid, precision=precise)
    return jnp.einsum("mib,bj->mij", backward_grid, column_sine, precision=precise)


def shards(data_vec, kernel, time_spectrum, prior_spectrum, noise_var):
    tm_index = lax.axis_index("tm")
    stripes = lax.axis_size("stripe")
    steps_here = data_vec.shape[0]
    vectors = data_vec.shape[1]
    freqs_here = kernel.shape[0]
    points_here = kernel.shape[3]
    time_total = steps_here * lax.axis_size("tm")
    rows_all = prior_spectrum.shape[0]
    columns = prior_spectrum.shape[1]
    rows_here = points_here // columns
    data_all = lax.all_gather(data_vec, "stripe", axis=2, tiled=True)
    summed = lax.psum_scatter(
        spectra_term(data_all, tm_index, time_total, freqs_here * lax.axis_size("tm")),
        "tm",
        scatter_dimension=0,
        tiled=True,
    )
    spectra = summed.astype(jnp.bfloat16)
    swapped = jnp.stack([spectra[:, 1], -spectra[:, 0]], 1)
    adj_real = jnp.einsum("kcsp,kcns->knp", kernel, spectra, preferred_element_type=jnp.float32)
    adj_imag = jnp.einsum("kcsp,kcns->knp", kernel, swapped, preferred_element_type=jnp.float32)
    adjoint = jnp.stack([adj_real, adj_imag], 1) * time_spectrum[:, None, None, None]
    row_sine = sine_matrix(rows_all)
    column_sine = sine_matrix(columns)
    item_count = freqs_here * 2 * vectors
    per_group = item_count // stripes
    grid_stack = adjoint.reshape(stripes, per_group, rows_here, columns)
    shaped = grid_prior(
        lax.all_to_all(grid_stack, "stripe", split_axis=0, concat_axis=2, tiled=True)[0],
        row_sine,
        column_sine,
        prior_spectrum,
    )
    smoothed = lax.all_to_all(
        shaped[None].astype(jnp.bfloat16), "stripe", split_axis=2, concat_axis=0, tiled=True
    ).astype(jnp.float32)
    smoothed_bf = smoothed.reshape(freqs_here, 2, vectors, points_here).astype(jnp.bfloat16)
    pair_real = jnp.stack([smoothed_bf[:, 0], -smoothed_bf[:, 1]], 1)
    pair_imag = jnp.stack([smoothed_bf[:, 1], smoothed_bf[:, 0]], 1)
    out_real = jnp.einsum("kcsp,kcnp->kns", kernel, pair_real, preferred_element_type=jnp.float32)
    out_imag = jnp.einsum("kcsp,kcnp->kns", kernel, pair_imag, preferred_element_type=jnp.float32)
    images = jnp.stack([out_real, out_imag], 1)
    time_sums = lax.psum_scatter(
        times_term(images, tm_index, time_total, steps_here * lax.axis_size("tm")),
        "tm",
        scatter_dimension=0,
        tiled=True,
    )
    result = lax.psum_scatter(time_sums, "stripe", scatter_dimension=2, tiled=True)
    return result + noise_var[None, None, :] * data_vec


def solution(mesh):
    return jax.shard_map(
        shards,
        mesh=mesh,
        in_specs=(
            P("tm", None, "stripe"),
            P("tm", None, None, "stripe"),
            P("tm"),
            P(),
            P("stripe"),
        ),
        out_specs=P("tm", None, "stripe"),
        check_vma=False,
    )
```

profile of v0, /device:TPU:4, one launch (start us, length us, event | category | flops | bytes accessed | tf_op | source)
XLA Modules:
  0.0 538.7 jit_solution(7578918533974694577)
XLA Ops:
  6.5 0.8 copy.22
  7.3 29.1 %all_gather.3 = f32[4,2,512]{0,1,2:T(2,128)S(1)} all-gather(f32[4,2,64]{0,1,2:T(2,128)S(1)} %copy.22), channel_id=1, replica_groups=mesh['tm'=32,'stripe'=8] {'stripe'}, dimensions={2}, use_global_device_ids=true | all-gather | bytes 18432 | tf_op jit(solution)/shard_map/all_gather | solution.py:64
  36.7 0.8 convolution_bitcast_fusion
  37.4 0.7 fusion.1
  38.3 139.7 %all-reduce.6 = bf16[128,2,2,512]{3,0,2,1:T(8,128)(2,1)S(1)} all-reduce(f32[128,2,2,512]{3,0,2,1:T(8,128)S(1)} %maximum_multiply_fusion), channel_id=2, replica_groups=mesh['tm'=32,'stripe'=8] {'tm'}, use_global_device_ids=true, to_apply=%region_0.1.clone | all-reduce | flops 262144 | bytes 1572864
  178.0 1.3 dynamic-slice
  180.0 4.7 convolution_bitcast_fusion.4
  184.8 0.9 copy-done
  185.7 1.2 convolution_bitcast_fusion.3
  187.3 0.7 reshape.53
  188.1 5.3 all-to-all-start
  193.4 6.3 %all-to-all-done = f32[8,1,2048]{2,1,0:T(1,128)S(1)} async-done(((f32[8,1,2048]{2,1,0:T(1,128)}), f32[8,1,2048]{2,1,0:T(1,128)S(1)}, u32[]{:S(2)}, u32[]{:S(2)}) %all-to-all-start) | async-done | bytes 65568 | tf_op jit(solution)/shard_map/all_to_all | solution.py:82
  200.2 0.8 reduce
  203.3 8.7 %all_to_all.33 = bf16[8,2,1024]{2,1,0:T(2,128)(2,1)S(1)} all-to-all(bf16[8,2,1024]{2,1,0:T(2,128)(2,1)S(1)} %reshape.55), channel_id=1, replica_groups=mesh['tm'=32,'stripe'=8] {'stripe'}, dimensions={0} | all-to-all | bytes 65536 | tf_op jit(solution)/shard_map/all_to_all | solution.py:87
  212.4 5.7 %convolution_bitcast_fusion.6 = f32[4,2,512]{2,1,0:T(2,128)S(1)} fusion(bf16[4,2,512,1024]{3,2,1,0:T(8,128)(2,1)} %param.6, bf16[4,1,2,1024]{3,2,1,0:T(2,128)(2,1)S(1)} %get-tuple-element.5, bf16[4,1,2,1024]{3,2,1,0:T(2,128)(2,1)S(1)} %copy.48), kind=kOutput, calls=%fused_computation.13 | convolution fusion | flops 16842752 | bytes 8437760 | tf_op jit(solution)/shard_map/kcsp,kcnp->kns/dot_general | solution.py:93
  218.0 0.8 fusion.45
  218.8 5.7 %convolution_bitcast_fusion.5 = f32[4,2,512]{2,1,0:T(2,128)S(1)} fusion(bf16[4,2,512,1024]{3,2,1,0:T(8,128)(2,1)} %param.6, bf16[4,1,2,1024]{3,2,1,0:T(2,128)(2,1)S(1)} %copy.48, bf16[4,1,2,1024]{3,2,1,0:T(2,128)(2,1)S(1)} %get-tuple-element.6), kind=kOutput, calls=%fused_computation.12 | convolution fusion | flops 16842752 | bytes 8437760 | tf_op jit(solution)/shard_map/kcsp,kcnp->kns/dot_general | solution.py:94
  224.5 1.6 fusion
  226.1 262.5 %all-reduce.5.cloned.1.call-done = f32[128,2,512]{2,0,1:T(8,128)} async-done(((f32[128,2,512]{2,0,1:T(8,128)}), f32[128,2,512]{2,0,1:T(8,128)}) %all-reduce.5.cloned.1.call-update) | async-done | bytes 524304
  488.6 0.8 constant_dynamic-slice_fusion
  489.6 1.0 reshape.49
  490.6 39.7 %reduce-scatter.6.cloned.1.call-done = f32[64,8]{1,0:T(8,128)} async-done(((f32[512,8]{1,0:T(8,128)}), f32[64,8]{1,0:T(8,128)}) %reduce-scatter.6.cloned.1.call-update) | async-done | bytes 2064
  530.3 0.9 reshape.50
  531.3 0.6 copy.35
  (45 shorter events, 4.4 us)
Async XLA Ops:
  179.9 5.8 %copy-start = (bf16[4,2,512,1024]{3,2,1,0:T(8,128)(2,1)S(1)}, bf16[4,2,512,1024]{3,2,1,0:T(8,128)(2,1)}, u32[]{:S(2)}) copy-start(bf16[4,2,512,1024]{3,2,1,0:T(8,128)(2,1)} %param.6) | copy-start | bytes 25165828
  180.0 7.1 %copy-start.3 = (f32[4]{0:T(128)S(1)}, f32[4]{0:T(128)}, u32[]{:S(2)}) copy-start(f32[4]{0:T(128)} %param.7) | copy-start | bytes 52
  180.0 21.7 %copy-start.1 = (f32[128,64]{0,1:T(8,128)S(1)}, f32[128,64]{0,1:T(8,128)}, u32[]{:S(2)}) copy-start(f32[128,64]{0,1:T(8,128)} %param.8) | copy-start | bytes 98308
  188.1 11.6 %all-to-all-start = ((f32[8,1,2048]{2,1,0:T(1,128)}), f32[8,1,2048]{2,1,0:T(1,128)S(1)}, u32[]{:S(2)}, u32[]{:S(2)}) async-start(f32[8,1,2048]{2,1,0:T(1,128)} %reshape.53), calls=%async_computation | async-start | bytes 131072 | tf_op jit(solution)/shard_map/all_to_all | solution.py:82
  193.4 295.2 %all-reduce.5.cloned.1.call-start = ((), (), s32[]{:S(2)}) async-start(), calls=%async_computation.4 | async-start | bytes 1048576
  212.4 318.9 %copy-start.2 = (f32[4,2,64]{2,1,0:T(2,128)S(1)}, f32[4,2,64]{2,1,0:T(2,128)}, u32[]{:S(2)}) copy-start(f32[4,2,64]{2,1,0:T(2,128)} %param.5) | copy-start | bytes 6148
  212.4 318.9 %copy-start.4 = (f32[64]{0:T(128)S(1)}, f32[64]{0:T(128)}, u32[]{:S(2)}) copy-start(f32[64]{0:T(128)} %param.9) | copy-start | bytes 772
  226.0 304.3 %reduce-scatter.6.cloned.1.call-start = ((), (), s32[]{:S(2)}) async-start(), calls=%async_computation.3 | async-start | bytes 294912
Sparse Core Ops, SparseCore 0:
  226.2 262.3 all-reduce.4
  491.1 39.2 reduce-scatter.5
where the time goes:
time: 539 us
  waiting for transfers between devices  308 us (57%)
  blocking collectives  177 us (33%)
  matrix products  23 us (4%)
  between operations  14.3 us (3%)
  local copies, waits for them, and re-layouts  9.02 us (2%)
    unnamed x4, waiting for transfers between devices  302 us
    unnamed x1, blocking collectives  140 us
    all_gather x1, blocking collectives, shards(): data_all = lax.all_gather(data_vec, 'stripe', axis=2, tiled=True)  29.1 us
  transfers between devices with their start and end apart: 3, of which 3 were waited for; matrix products, arithmetic and copies ran while one was open for 0% of the time, Pallas kernels for 0%

commit v1 on v0

--- a/solution.py
+++ b/solution.py
@@ -61,7 +61,9 @@
     rows_all = prior_spectrum.shape[0]
     columns = prior_spectrum.shape[1]
     rows_here = points_here // columns
-    data_all = lax.all_gather(data_vec, "stripe", axis=2, tiled=True)
+    data_all = jnp.concatenate(
+        lax.all_to_all(jnp.stack([data_vec] * lax.axis_size("stripe")), "stripe", 0, 0), axis=2
+    )
     summed = lax.psum_scatter(
         spectra_term(data_all, tm_index, time_total, freqs_here * lax.axis_size("tm")),
         "tm",

time: 539 us -> 522 us (0.968)
  blocking collectives: 177 us -> 152 us
    all_gather x1 -> x0, blocking collectives: 29.1 us -> none  [shards(): data_all = lax.all_gather(data_vec, 'stripe', axis=2, tiled=True)]
  transfers between devices with their start and end apart: 3 -> 4, of which waited for: 3 -> 4; matrix products, arithmetic and copies ran while one was open for 0% -> 0% of each run, Pallas kernels for 0% -> 0%
where the time goes in v1:
time: 522 us
  waiting for transfers between devices  312 us (60%)
  blocking collectives  152 us (29%)
  matrix products  23 us (4%)
  between operations  14.3 us (3%)
  local copies, waits for them, and re-layouts  10.2 us (2%)
  starting transfers between devices  8.9 us (2%)
    unnamed x4, waiting for transfers between devices  302 us
    unnamed x1, blocking collectives  143 us
  transfers between devices with their start and end apart: 4, of which 4 were waited for; matrix products, arithmetic and copies ran while one was open for 0% of the time, Pallas kernels for 0%

profile of v1, /device:TPU:4, one launch (start us, length us, event | category | flops | bytes accessed | tf_op | source)
XLA Modules:
  0.0 521.8 jit_solution(7382762255527206914)
XLA Ops:
  7.9 5.1 all-to-all-start
  13.1 0.7 mul.152
  13.9 1.3 dynamic-slice
  15.8 3.5 all-to-all-done
  20.6 0.7 convolution_bitcast_fusion
  21.4 0.7 fusion.1
  22.3 142.9 %all-reduce.6 = bf16[128,2,2,512]{3,0,2,1:T(8,128)(2,1)S(1)} all-reduce(f32[128,2,2,512]{3,0,2,1:T(8,128)S(1)} %maximum_multiply_fusion), channel_id=2, replica_groups=mesh['tm'=32,'stripe'=8] {'tm'}, use_global_device_ids=true, to_apply=%region_0.1.clone | all-reduce | flops 262144 | bytes 1572864
  165.3 4.7 convolution_bitcast_fusion.4
  170.0 0.9 copy-done
  171.0 1.2 convolution_bitcast_fusion.3
  172.5 0.7 reshape.65
  173.2 3.7 all-to-all-start.1
  177.0 6.3 %all-to-all-done.1 = f32[8,1,2048]{2,1,0:T(1,128)S(1)} async-done(((f32[8,1,2048]{2,1,0:T(1,128)}), f32[8,1,2048]{2,1,0:T(1,128)S(1)}, u32[]{:S(2)}, u32[]{:S(2)}) %all-to-all-start.1) | async-done | bytes 65568 | tf_op jit(solution)/shard_map/all_to_all | solution.py:84
  183.3 0.8 reduce.1
  186.3 8.7 %all_to_all.38 = bf16[8,2,1024]{2,1,0:T(2,128)(2,1)S(1)} all-to-all(bf16[8,2,1024]{2,1,0:T(2,128)(2,1)S(1)} %reshape.67), channel_id=1, replica_groups=mesh['tm'=32,'stripe'=8] {'stripe'}, dimensions={0} | all-to-all | bytes 65536 | tf_op jit(solution)/shard_map/all_to_all | solution.py:89
  195.4 5.7 %convolution_bitcast_fusion.6 = f32[4,2,512]{2,1,0:T(2,128)S(1)} fusion(bf16[4,2,512,1024]{3,2,1,0:T(8,128)(2,1)} %param.6, bf16[4,1,2,1024]{3,2,1,0:T(2,128)(2,1)S(1)} %get-tuple-element.5, bf16[4,1,2,1024]{3,2,1,0:T(2,128)(2,1)S(1)} %copy.47), kind=kOutput, calls=%fused_computation.13 | convolution fusion | flops 16842752 | bytes 8437760 | tf_op jit(solution)/shard_map/kcsp,kcnp->kns/dot_general | solution.py:95
  201.1 0.8 fusion.45
  201.8 5.7 %convolution_bitcast_fusion.5 = f32[4,2,512]{2,1,0:T(2,128)S(1)} fusion(bf16[4,2,512,1024]{3,2,1,0:T(8,128)(2,1)} %param.6, bf16[4,1,2,1024]{3,2,1,0:T(2,128)(2,1)S(1)} %copy.47, bf16[4,1,2,1024]{3,2,1,0:T(2,128)(2,1)S(1)} %get-tuple-element.6), kind=kOutput, calls=%fused_computation.12 | convolution fusion | flops 16842752 | bytes 8437760 | tf_op jit(solution)/shard_map/kcsp,kcnp->kns/dot_general | solution.py:96
  207.5 1.6 fusion
  209.1 262.5 %all-reduce.5.cloned.1.call-done = f32[128,2,512]{2,0,1:T(8,128)} async-done(((f32[128,2,512]{2,0,1:T(8,128)}), f32[128,2,512]{2,0,1:T(8,128)}) %all-reduce.5.cloned.1.call-update) | async-done | bytes 524304
  471.6 0.8 constant_dynamic-slice_fusion
  472.6 1.0 reshape.59
  473.7 39.7 %reduce-scatter.6.cloned.1.call-done = f32[64,8]{1,0:T(8,128)} async-done(((f32[512,8]{1,0:T(8,128)}), f32[64,8]{1,0:T(8,128)}) %reduce-scatter.6.cloned.1.call-update) | async-done | bytes 2064
  513.4 0.9 reshape.60
  (50 shorter events, 6.9 us)
Async XLA Ops:
  7.9 11.3 %all-to-all-start = ((f32[8,1,512]{2,1,0:T(1,128)}), f32[8,1,512]{2,1,0:T(1,128)S(1)}, u32[]{:S(2)}, u32[]{:S(2)}) async-start(f32[8,1,512]{2,1,0:T(1,128)} %reshape.63), calls=%async_computation | async-start | bytes 32768 | tf_op jit(solution)/shard_map/all_to_all | solution.py:65
  165.2 5.8 %copy-start = (bf16[4,2,512,1024]{3,2,1,0:T(8,128)(2,1)S(1)}, bf16[4,2,512,1024]{3,2,1,0:T(8,128)(2,1)}, u32[]{:S(2)}) copy-start(bf16[4,2,512,1024]{3,2,1,0:T(8,128)(2,1)} %param.6) | copy-start | bytes 25165828
  165.3 19.4 %copy-start.1 = (f32[128,64]{0,1:T(8,128)S(1)}, f32[128,64]{0,1:T(8,128)}, u32[]{:S(2)}) copy-start(f32[128,64]{0,1:T(8,128)} %param.8) | copy-start | bytes 98308
  173.2 10.1 %all-to-all-start.1 = ((f32[8,1,2048]{2,1,0:T(1,128)}), f32[8,1,2048]{2,1,0:T(1,128)S(1)}, u32[]{:S(2)}, u32[]{:S(2)}) async-start(f32[8,1,2048]{2,1,0:T(1,128)} %reshape.65), calls=%async_computation.1 | async-start | bytes 131072 | tf_op jit(solution)/shard_map/all_to_all | solution.py:84
  176.9 294.7 %all-reduce.5.cloned.1.call-start = ((), (), s32[]{:S(2)}) async-start(), calls=%async_computation.5 | async-start | bytes 1048576
  195.4 318.9 %copy-start.2 = (f32[4,2,64]{2,1,0:T(2,128)S(1)}, f32[4,2,64]{2,1,0:T(2,128)}, u32[]{:S(2)}) copy-start(f32[4,2,64]{2,1,0:T(2,128)} %param.5) | copy-start | bytes 6148
  195.4 318.9 %copy-start.3 = (f32[64]{0:T(128)S(1)}, f32[64]{0:T(128)}, u32[]{:S(2)}) copy-start(f32[64]{0:T(128)} %param.9) | copy-start | bytes 772
  209.1 304.3 %reduce-scatter.6.cloned.1.call-start = ((), (), s32[]{:S(2)}) async-start(), calls=%async_computation.4 | async-start | bytes 294912
Sparse Core Ops, SparseCore 0:
  209.2 262.3 all-reduce.4
  474.1 39.2 reduce-scatter.5
